TPU v7x, 32 devices: a whole 2x2x4 slice. The times are simulated.
32 devices in a mesh: req: 8 (over z, x), mp: 4 (over y, core).
Axes of the slice: x: 2, y: 2, z: 4, core: 2. Of those that a mesh axis runs over, the one named last changes fastest.
Arguments:
- hidden: bfloat16 [2048, 4096], P(('req', 'mp')), may hold values from -4 to 4
- queries: bfloat16 [2048, 2048], P('req', 'mp'), may hold values from -130 to 130
- rotated_rollout_keys: bfloat16 [2048, 2, 128], P('req'), may hold values from -4 to 4
- rollout_value_matrix: bfloat16 [2048, 2, 128], P('req'), may hold values from -4 to 4
- cached_key_slabs: bfloat16 [16384, 2, 128], P('req'), may hold values from -4 to 4
- cached_value_slabs: bfloat16 [16384, 2, 128], P('req'), may hold values from -4 to 4
- out_weight: bfloat16 [2048, 4096], P('mp'), may hold values from -0.5 to 0.5
- final_gain: float32 [4096], replicated, may hold values from 0.1 to 1.9
- head_weight: bfloat16 [4096, 32000], P(None, 'req'), may hold values from -1 to 1
- token_ids: int32 [2048], P(('req', 'mp')), may hold values from 0 to 31999
- rollout_len: int32 [8], P('req'), may hold values from 64 to 256
- piece_offset: int32 [8], P('req'), may hold values from 0 to 3
- piece_len: int32 [8], P('req'), may hold values from 256 to 2048
Outputs:
- logprob: float32 [2048], P(('req', 'mp'))
- entropy: float32 [2048], P(('req', 'mp'))
All inputs are finite; a program needn't handle non-finite values.
Results may differ from a plain program's by a relative error of at most 0.0045.
Values may be sent and summed in bfloat16 or wider, within the bound.
No kernel may reach another device: no remote copies, remote signals or barrier semaphores. Data moves between devices by JAX's collectives and lax.ppermute only.
A program may use at most 128 MiB of HBM per device.

v0:
```python
import math
import jax
import jax.numpy as jnp
from jax import lax
from jax.sharding import PartitionSpec as P

REACH = 4
NEGATIVE = -1e30


def shifted(block, axis, distance):
    devices = range(lax.axis_size(axis))
    route = [((i - distance) % len(devices), i) for i in devices]
    return lax.ppermute(block, axis, route)


def combined_all(shard, axis, combine):
    everything = jax.tree.map(lambda part: lax.all_gather(part, axis), shard)
    leading = jax.tree.map(lambda part: part[0], everything)

    def hop(k, so_far):
        return combine(so_far, jax.tree.map(lambda part: part[k], everything))

    return lax.fori_loop(1, lax.axis_size(axis), hop, leading)


def partial_softmax(query, keys, values, mask, factor):
    scores = jnp.einsum("thd,cd->thc", query, keys, preferred_element_type=jnp.float32) * factor
    scores = jnp.where(mask[:, None, :], scores, NEGATIVE)
    top = jnp.max(scores, axis=-1)
    weights = jnp.exp(scores - top[..., None])
    total = jnp.sum(weights, axis=-1)
    summed = jnp.einsum(
        "thc,cd->thd", weights.astype(jnp.bfloat16), values, preferred_element_type=jnp.float32
    )
    return (top, total, summed)


def join_parts(parts):
    tops = jnp.concatenate([item[0] for item in parts], axis=0)
    totals = jnp.concatenate([item[1] for item in parts], axis=0)
    sums = jnp.concatenate([item[2] for item in parts], axis=0)
    highest = jnp.max(tops, axis=0)
    scales = jnp.exp(tops - highest[None])
    total = jnp.sum(totals * scales, axis=0)
    summed = jnp.einsum("nth,nthd->thd", scales, sums)
    return summed / total[..., None]


def merge_summary(leading_slab, second):
    highest = jnp.maximum(leading_slab[0], second[0])
    left = jnp.exp(leading_slab[0] - highest)
    right = jnp.exp(second[0] - highest)
    return (
        highest,
        leading_slab[1] * left + second[1] * right,
        leading_slab[2] * left + second[2] * right,
        leading_slab[3] + second[3],
    )


def body(
    hidden,
    queries,
    rotated_rollout_keys,
    rollout_value_matrix,
    cached_key_slabs,
    cached_value_slabs,
    out_weight,
    final_gain,
    head_weight,
    token_ids,
    rollout_len,
    piece_offset,
    piece_len,
):
    groups = lax.axis_size("req")
    request = lax.axis_index("req")
    shard = lax.axis_index("mp")
    rollout = queries.shape[0]
    head_size = rotated_rollout_keys.shape[2]
    heads_here = queries.shape[1] // head_size
    group_size = heads_here * lax.axis_size("mp") // rotated_rollout_keys.shape[1]
    value_head = shard * heads_here // group_size
    factor = 1.0 / math.sqrt(head_size)
    offset = piece_offset[0]
    current_slab_keys = lax.dynamic_index_in_dim(cached_key_slabs, value_head, 1, keepdims=False)
    current_slab_values = lax.dynamic_index_in_dim(
        cached_value_slabs, value_head, 1, keepdims=False
    )
    slab_valid = jnp.arange(cached_key_slabs.shape[0]) < piece_len[0]
    rollout_key_rows = lax.dynamic_index_in_dim(rotated_rollout_keys, value_head, 1, keepdims=False)
    rollout_value_rows = lax.dynamic_index_in_dim(
        rollout_value_matrix, value_head, 1, keepdims=False
    )
    rows = jnp.arange(rollout)
    causal = rows[None, :] <= rows[:, None]
    own_query = queries.reshape(rollout, heads_here, head_size)
    local = partial_softmax(own_query, rollout_key_rows, rollout_value_rows, causal, factor)
    parts = [tuple((item[None] for item in local))]
    slab_mask = jnp.broadcast_to(slab_valid, (rollout, cached_key_slabs.shape[0]))
    visitor = queries
    for step in range(1, REACH):
        moved = shifted(queries, "req", step)
        visitor = jnp.where(offset == step, moved, visitor)
    top, total, summed = partial_softmax(
        visitor.reshape(rollout, heads_here, head_size),
        current_slab_keys,
        current_slab_values,
        slab_mask,
        factor,
    )
    keep = offset == 0
    parts.append(
        (
            jnp.where(keep, top, NEGATIVE)[None],
            jnp.where(keep, total, 0.0)[None],
            jnp.where(keep, summed, 0.0)[None],
        )
    )
    for step in range(1, REACH):
        mine = offset == step
        back_sum, back_top, back_total = shifted(
            (
                jnp.where(mine, summed, 0.0),
                jnp.where(mine, top, NEGATIVE),
                jnp.where(mine, total, 0.0),
            ),
            "req",
            -step,
        )
        parts.append((back_top[None], back_total[None], back_sum[None]))
    mixed = join_parts(parts).astype(jnp.bfloat16).reshape(rollout, heads_here * head_size)
    rows_here = hidden.shape[0]
    block = mixed
    added = lax.psum_scatter(
        jnp.dot(block, out_weight, preferred_element_type=jnp.float32),
        "mp",
        scatter_dimension=0,
        tiled=True,
    )
    stream = hidden.astype(jnp.float32) + added
    normed = (
        stream * lax.rsqrt(jnp.mean(stream * stream, axis=-1, keepdims=True) + 1e-06) * final_gain
    ).astype(jnp.bfloat16)
    vocabulary_here = head_weight.shape[1]
    first_word = request * vocabulary_here
    columns = jnp.arange(vocabulary_here)
    block = lax.all_gather(normed, "req", axis=0, tiled=True)
    words = lax.all_gather(token_ids, "req", axis=0, tiled=True)
    logits = jnp.dot(block, head_weight, preferred_element_type=jnp.float32)
    highest = jnp.max(logits, axis=-1)
    spread = jnp.exp(logits - highest[:, None])
    total = jnp.sum(spread, axis=-1)
    weighted = jnp.sum(spread * logits, axis=-1)
    picked = jnp.sum(
        jnp.where(columns[None, :] == (words - first_word)[:, None], logits, 0.0), axis=-1
    )
    fresh = (highest, total, weighted, picked)
    summary = tuple((fresh[index] for index in range(4)))
    table = tuple((item.reshape(groups, rows_here) for item in summary))
    pooled = combined_all(table, "req", merge_summary)
    highest, total, weighted, picked = (
        lax.dynamic_index_in_dim(item, request, 0, keepdims=False) for item in pooled
    )
    log_total = highest + jnp.log(total)
    positions = shard * rows_here + jnp.arange(rows_here)
    valid = positions < rollout_len[0]
    logprob = jnp.where(valid, picked - log_total, 0.0)
    entropy = jnp.where(valid, log_total - weighted / total, 0.0)
    return (logprob, entropy)


def solution(mesh):
    placed = (
        P(("req", "mp"), None),
        P("req", "mp"),
        P("req", None, None),
        P("req", None, None),
        P("req", None, None),
        P("req", None, None),
        P("mp", None),
        P(),
        P(None, "req"),
        P(("req", "mp")),
        P("req"),
        P("req"),
        P("req"),
    )
    return jax.shard_map(
        body,
        mesh=mesh,
        in_specs=placed,
        out_specs=(P(("req", "mp")), P(("req", "mp"))),
        check_vma=False,
    )
```

profile of v0, /device:TPU:0, one launch (start us, length us, event | category | flops | bytes accessed | tf_op | source)
XLA Modules:
  0.0 363.0 jit_solution(10148285551743144967)
XLA Ops:
  7.2 4.0 %collective-permute-start = (bf16[256,512]{1,0:T(8,128)(2,1)}, bf16[256,512]{1,0:T(8,128)(2,1)S(1)}, u32[]{:S(2)}, u32[]{:S(2)}) collective-permute-start(bf16[256,512]{1,0:T(8,128)(2,1)} %param.16), channel_id=1, source_target_pairs={{20,0},{24,4},{28,8},{0,12},{4,16},{8,20},{12,24},{16,28},{21,1},{... | collective-permute-start | bytes 786440 | tf_op jit(solution)/shard_map/ppermute | solution.py:14
  11.2 1.6 collective-permute-start.1
  12.8 1.5 collective-permute-start.2
  15.7 1.1 constant_dynamic-slice_fusion.6
  16.9 1.0 constant_dynamic-slice_fusion.7
  17.9 1.3 fusion.34
  19.2 0.2 fusion.15
  19.4 1.0 constant_dynamic-slice_fusion.5
  20.5 2.2 constant_dynamic-slice_fusion.4
  22.6 0.3 fusion.14
  23.0 12.6 %collective-permute-done = bf16[256,512]{1,0:T(8,128)(2,1)S(1)} collective-permute-done((bf16[256,512]{1,0:T(8,128)(2,1)}, bf16[256,512]{1,0:T(8,128)(2,1)S(1)}, u32[]{:S(2)}, u32[]{:S(2)}) %collective-permute-start) | collective-permute-done | bytes 262176 | tf_op jit(solution)/shard_map/ppermute | solution.py:14
  35.6 1.6 fusion.4
  37.2 1.9 fusion.5
  39.2 1.1 collective-permute-start.10
  40.3 3.0 collective-permute-start.11
  43.3 1.5 collective-permute-start.3
  44.8 0.3 collective-permute-start.4
  45.1 2.0 bitcast_dynamic-update-slice_fusion.3
  47.1 0.2 broadcast_select_fusion
  47.3 3.2 collective-permute-start.5
  50.5 1.9 collective-permute-start.6
  52.4 2.7 collective-permute-start.7
  55.1 1.0 collective-permute-start.8
  56.2 0.1 copy.32
  56.3 0.4 copy.34
  56.7 2.4 collective-permute-done.6
  59.2 5.6 %collective-permute-done.7 = bf16[256,4,128]{2,0,1:T(8,128)(2,1)S(1)} collective-permute-done((bf16[256,4,128]{2,0,1:T(8,128)(2,1)S(1)}, bf16[256,4,128]{2,0,1:T(8,128)(2,1)S(1)}, u32[]{:S(2)}, u32[]{:S(2)}) %collective-permute-start.7) | collective-permute-done | bytes 262176 | tf_op jit(solution)/shard_map/ppermute | solution.py:14
  64.8 3.2 collective-permute-done.8
  68.1 1.3 fusion.7
  69.4 0.3 divide_convert_fusion
  69.8 5.4 %fusion.20 = f32[256,4096]{1,0:T(8,128)} fusion(bf16[512,4096]{1,0:T(8,128)(2,1)} %param.21, bf16[32,8,4,128]{3,2,1,0:T(4,128)(2,1)S(1)} %bitcast.137), kind=kOutput, calls=%fused_computation.43 | convolution fusion | flops 1073741824 | bytes 8650752 | tf_op jit(solution)/shard_map/dot_general | solution.py:137
  75.2 0.2 all-gather.2.cloned.1.call-start
  75.5 51.9 %reduce-scatter.2.cloned.1.call-done = f32[64,4096]{1,0:T(8,128)} async-done(((f32[256,4096]{1,0:T(8,128)}), f32[64,4096]{1,0:T(8,128)}) %reduce-scatter.2.cloned.1.call-update) | async-done | bytes 1048592 | tf_op jit(solution)/shard_map/reduce_scatter | solution.py:136
  127.4 1.5 multiply_reduce_fusion.1
  128.9 2.2 multiply_convert_fusion
  131.8 0.6 dynamic-slice
  133.0 0.2 dynamic-update-slice
  133.3 11.8 %all-reduce = s32[512]{0:T(512)S(1)} all-reduce(s32[512]{0:T(512)S(1)} %dynamic-update-slice), channel_id=1, replica_groups=mesh['req'=8,'mp'=4] {'req'}, use_global_device_ids=true, to_apply=%add | all-reduce | flops 512 | bytes 4096
  145.1 59.6 %all-gather.2.cloned.1.call-done = bf16[512,4096]{1,0:T(8,128)(2,1)} async-done(((bf16[64,4096]{1,0:T(8,128)(2,1)}), bf16[512,4096]{1,0:T(8,128)(2,1)}) %all-gather.2.cloned.1.call-update) | async-done | bytes 4194320 | tf_op jit(solution)/shard_map/all_gather | solution.py:149
  204.7 23.6 %fusion.35 = (f32[512]{0:T(512)S(1)}, f32[512,4000]{0,1:T(8,128)}) fusion(bf16[512,4096]{1,0:T(8,128)(2,1)} %all-gather.2.cloned.1.call-done, bf16[4096,4000]{0,1:T(8,128)(2,1)} %param.23), kind=kOutput, calls=%fused_computation.102 | convolution fusion | flops 16779264000 | bytes 45156352 | tf_op jit(solution)/shard_map/dot_general | solution.py:151
  228.3 0.1 all_gather_reshape.12
  228.4 4.8 %multiply_reduce_fusion = (f32[512]{0:T(512)S(1)}, f32[512]{0:T(512)S(1)}, f32[512]{0:T(512)S(1)}) fusion(f32[512,4000]{0,1:T(8,128)} %get-tuple-element.271, f32[512]{0:T(512)S(1)} %get-tuple-element.270, s32[512]{0:T(512)S(1)} %broadcast_subtract_fusion), kind=kLoop, calls=%fused_computation.13 | loop fusion | flops 14334464 | bytes 8202240 | tf_op jit(solution)/shard_map/reduce_sum | solution.py:155
  233.3 30.4 %all_gather.23 = f32[8,8,64]{2,1,0:T(8,128)S(1)} all-gather(f32[1,8,64]{2,1,0:T(8,128)S(1)} %all_gather_reshape.15), channel_id=1, replica_groups=mesh['req'=8,'mp'=4] {'req'}, dimensions={0}, use_global_device_ids=true | all-gather | bytes 18432 | tf_op jit(solution)/shard_map/all_gather | solution.py:18
  263.8 30.4 %all_gather.21 = f32[8,8,64]{2,1,0:T(8,128)S(1)} all-gather(f32[1,8,64]{2,1,0:T(8,128)S(1)} %all_gather_reshape.14), channel_id=1, replica_groups=mesh['req'=8,'mp'=4] {'req'}, dimensions={0}, use_global_device_ids=true | all-gather | bytes 18432 | tf_op jit(solution)/shard_map/all_gather | solution.py:18
  294.3 30.4 %all_gather.20 = f32[8,8,64]{2,1,0:T(8,128)S(1)} all-gather(f32[1,8,64]{2,1,0:T(8,128)S(1)} %all_gather_reshape.13), channel_id=1, replica_groups=mesh['req'=8,'mp'=4] {'req'}, dimensions={0}, use_global_device_ids=true | all-gather | bytes 18432 | tf_op jit(solution)/shard_map/all_gather | solution.py:18
  324.7 30.4 %all_gather.19 = f32[8,8,64]{2,1,0:T(8,128)S(1)} all-gather(f32[1,8,64]{2,1,0:T(8,128)S(1)} %all_gather_reshape.12), channel_id=1, replica_groups=mesh['req'=8,'mp'=4] {'req'}, dimensions={0}, use_global_device_ids=true | all-gather | bytes 18432 | tf_op jit(solution)/shard_map/all_gather | solution.py:18
  355.1 0.5 while.21
  355.6 0.5 compare_select_fusion
  (77 shorter events, 1.0 us)
Async XLA Ops:
  7.2 8.6 %copy-start = (bf16[2048,2,128]{2,1,0:T(2,128)(2,1)S(1)}, bf16[2048,2,128]{2,1,0:T(2,128)(2,1)}, u32[]{:S(2)}) copy-start(bf16[2048,2,128]{2,1,0:T(2,128)(2,1)} %param.19) | copy-start | bytes 3145732
  7.2 28.5 %copy-start.3 = (bf16[256,512]{1,0:T(8,128)(2,1)S(1)}, bf16[256,512]{1,0:T(8,128)(2,1)}, u32[]{:S(2)}) copy-start(bf16[256,512]{1,0:T(8,128)(2,1)} %param.16) | copy-start | bytes 786436
  7.2 120.2 %reduce-scatter.2.cloned.1.call-start = ((), (), s32[]{:S(2)}) async-start(), calls=%async_computation.1 | async-start | bytes 5242880 | tf_op jit(solution)/shard_map/reduce_scatter | solution.py:136
  7.2 28.4 %collective-permute-start = (bf16[256,512]{1,0:T(8,128)(2,1)}, bf16[256,512]{1,0:T(8,128)(2,1)S(1)}, u32[]{:S(2)}, u32[]{:S(2)}) collective-permute-start(bf16[256,512]{1,0:T(8,128)(2,1)} %param.16), channel_id=1, source_target_pairs={{20,0},{24,4},{28,8},{0,12},{4,16},{8,20},{12,24},{16,28},{21,1},{... | collective-permute-start | bytes 786440 | tf_op jit(solution)/shard_map/ppermute | solution.py:14
  11.2 24.4 %collective-permute-start.1 = (bf16[256,512]{1,0:T(8,128)(2,1)}, bf16[256,512]{1,0:T(8,128)(2,1)S(1)}, u32[]{:S(2)}, u32[]{:S(2)}) collective-permute-start(bf16[256,512]{1,0:T(8,128)(2,1)} %param.16), channel_id=1, source_target_pairs={{24,0},{28,4},{0,8},{4,12},{8,16},{12,20},{16,24},{20,28},{25,1},{... | collective-permute-start | bytes 786440 | tf_op jit(solution)/shard_map/ppermute | solution.py:14
  12.8 22.8 %collective-permute-start.2 = (bf16[256,512]{1,0:T(8,128)(2,1)}, bf16[256,512]{1,0:T(8,128)(2,1)S(1)}, u32[]{:S(2)}, u32[]{:S(2)}) collective-permute-start(bf16[256,512]{1,0:T(8,128)(2,1)} %param.16), channel_id=1, source_target_pairs={{28,0},{0,4},{4,8},{8,12},{12,16},{16,20},{20,24},{24,28},{29,1},{... | collective-permute-start | bytes 786440 | tf_op jit(solution)/shard_map/ppermute | solution.py:14
  39.1 16.0 %collective-permute-start.9 = (f32[256,4]{0,1:T(4,128)S(1)}, f32[256,4]{0,1:T(4,128)S(1)}, u32[]{:S(2)}, u32[]{:S(2)}) collective-permute-start(f32[256,4]{0,1:T(4,128)S(1)} %get-tuple-element.260), channel_id=1, source_target_pairs={{4,0},{8,4},{12,8},{16,12},{20,16},{24,20},{28,24},{0,28},{5,1},{9... | collective-permute-start | bytes 12296 | tf_op jit(solution)/shard_map/ppermute | solution.py:14
  39.2 16.9 %collective-permute-start.10 = (f32[256,4]{0,1:T(4,128)S(1)}, f32[256,4]{0,1:T(4,128)S(1)}, u32[]{:S(2)}, u32[]{:S(2)}) collective-permute-start(f32[256,4]{0,1:T(4,128)S(1)} %get-tuple-element.259), channel_id=1, source_target_pairs={{8,0},{12,4},{16,8},{20,12},{24,16},{28,20},{0,24},{4,28},{9,1},{1... | collective-permute-start | bytes 12296 | tf_op jit(solution)/shard_map/ppermute | solution.py:14
  40.3 15.8 %collective-permute-start.11 = (f32[256,4]{0,1:T(4,128)S(1)}, f32[256,4]{0,1:T(4,128)S(1)}, u32[]{:S(2)}, u32[]{:S(2)}) collective-permute-start(f32[256,4]{0,1:T(4,128)S(1)} %get-tuple-element.258), channel_id=1, source_target_pairs={{12,0},{16,4},{20,8},{24,12},{28,16},{0,20},{4,24},{8,28},{13,1},{... | collective-permute-start | bytes 12296 | tf_op jit(solution)/shard_map/ppermute | solution.py:14
  43.3 4.0 %collective-permute-start.3 = (f32[256,4]{0,1:T(4,128)S(1)}, f32[256,4]{0,1:T(4,128)S(1)}, u32[]{:S(2)}, u32[]{:S(2)}) collective-permute-start(f32[256,4]{0,1:T(4,128)S(1)} %get-tuple-element.263), channel_id=1, source_target_pairs={{4,0},{8,4},{12,8},{16,12},{20,16},{24,20},{28,24},{0,28},{5,1},{9... | collective-permute-start | bytes 12296 | tf_op jit(solution)/shard_map/ppermute | solution.py:14
  44.8 5.7 %collective-permute-start.4 = (f32[256,4]{0,1:T(4,128)S(1)}, f32[256,4]{0,1:T(4,128)S(1)}, u32[]{:S(2)}, u32[]{:S(2)}) collective-permute-start(f32[256,4]{0,1:T(4,128)S(1)} %get-tuple-element.262), channel_id=1, source_target_pairs={{8,0},{12,4},{16,8},{20,12},{24,16},{28,20},{0,24},{4,28},{9,1},{1... | collective-permute-start | bytes 12296 | tf_op jit(solution)/shard_map/ppermute | solution.py:14
  47.3 5.1 %collective-permute-start.5 = (f32[256,4]{0,1:T(4,128)S(1)}, f32[256,4]{0,1:T(4,128)S(1)}, u32[]{:S(2)}, u32[]{:S(2)}) collective-permute-start(f32[256,4]{0,1:T(4,128)S(1)} %get-tuple-element.261), channel_id=1, source_target_pairs={{12,0},{16,4},{20,8},{24,12},{28,16},{0,20},{4,24},{8,28},{13,1},{... | collective-permute-start | bytes 12296 | tf_op jit(solution)/shard_map/ppermute | solution.py:14
  50.5 8.7 %collective-permute-start.6 = (bf16[256,4,128]{2,0,1:T(8,128)(2,1)S(1)}, bf16[256,4,128]{2,0,1:T(8,128)(2,1)S(1)}, u32[]{:S(2)}, u32[]{:S(2)}) collective-permute-start(bf16[256,4,128]{2,0,1:T(8,128)(2,1)S(1)} %get-tuple-element.255), channel_id=1, source_target_pairs={{4,0},{8,4},{12,8},{16,12},{20,16},{24,20},{28,24},{0,28},{5,1},{9... | collective-permute-start | bytes 786440 | tf_op jit(solution)/shard_map/ppermute | solution.py:14
  52.4 12.4 %collective-permute-start.7 = (bf16[256,4,128]{2,0,1:T(8,128)(2,1)S(1)}, bf16[256,4,128]{2,0,1:T(8,128)(2,1)S(1)}, u32[]{:S(2)}, u32[]{:S(2)}) collective-permute-start(bf16[256,4,128]{2,0,1:T(8,128)(2,1)S(1)} %get-tuple-element.254), channel_id=1, source_target_pairs={{8,0},{12,4},{16,8},{20,12},{24,16},{28,20},{0,24},{4,28},{9,1},{1... | collective-permute-start | bytes 786440 | tf_op jit(solution)/shard_map/ppermute | solution.py:14
  55.1 12.9 %collective-permute-start.8 = (bf16[256,4,128]{2,0,1:T(8,128)(2,1)S(1)}, bf16[256,4,128]{2,0,1:T(8,128)(2,1)S(1)}, u32[]{:S(2)}, u32[]{:S(2)}) collective-permute-start(bf16[256,4,128]{2,0,1:T(8,128)(2,1)S(1)} %get-tuple-element.253), channel_id=1, source_target_pairs={{12,0},{16,4},{20,8},{24,12},{28,16},{0,20},{4,24},{8,28},{13,1},{... | collective-permute-start | bytes 786440 | tf_op jit(solution)/shard_map/ppermute | solution.py:14
  69.4 58.0 %copy-start.2 = (bf16[64,4096]{1,0:T(8,128)(2,1)S(1)}, bf16[64,4096]{1,0:T(8,128)(2,1)}, u32[]{:S(2)}) copy-start(bf16[64,4096]{1,0:T(8,128)(2,1)} %param.15) | copy-start | bytes 1572868
  69.8 59.1 %copy-start.4 = (f32[4096]{0:T(1024)S(1)}, f32[4096]{0:T(1024)}, u32[]{:S(2)}) copy-start(f32[4096]{0:T(1024)} %param.22) | copy-start | bytes 49156
  69.8 62.0 %copy-start.6 = (u32[32]{0:T(128)S(1)}, u32[32]{0:T(128)}, u32[]{:S(2)}) copy-start(u32[32]{0:T(128)} %constant.121) | copy-start | bytes 388
  69.8 63.2 %copy-start.5 = (s32[64]{0:T(128)S(1)}, s32[64]{0:T(128)}, u32[]{:S(2)}) copy-start(s32[64]{0:T(128)} %param.24) | copy-start | bytes 772
  75.2 129.4 %all-gather.2.cloned.1.call-start = ((), (), s32[]{:S(2)}) async-start(), calls=%async_computation.2 | async-start | bytes 4718592 | tf_op jit(solution)/shard_map/all_gather | solution.py:149
  204.7 151.5 %copy-start.1 = (bf16[2048,2,128]{2,1,0:T(2,128)(2,1)S(1)}, bf16[2048,2,128]{2,1,0:T(2,128)(2,1)}, u32[]{:S(2)}) copy-start(bf16[2048,2,128]{2,1,0:T(2,128)(2,1)} %param.19) | copy-start | bytes 3145732
Sparse Core Ops, SparseCore 0:
  75.4 51.9 reduce-scatter.1
  131.2 73.3 all-gather.1
where the time goes:
time: 363 us
  waiting for transfers between devices  135 us (37%)
  blocking collectives  133 us (37%)
  matrix products  35.6 us (10%)
  starting transfers between devices  22.1 us (6%)
  between operations  17 us (5%)
  other arithmetic  12 us (3%)
  local copies, waits for them, and re-layouts  7.34 us (2%)
    all_gather x4, blocking collectives, combined_all(): everything = jax.tree.map(lambda part: lax.all_gather(part, axis), shard)  122 us
    all_gather x1, waiting for transfers between devices, body(): block = lax.all_gather(normed, 'req', axis=0, tiled=True)  59.6 us
    reduce_scatter x1, waiting for transfers between devices, body(): lax.psum_scatter(jnp.dot(block, out_weight, preferred_element_type=jnp.fl...  51.9 us
    ppermute x12, waiting for transfers between devices, shifted(): return lax.ppermute(block, axis, route)  23.8 us
    dot_general x1, matrix products, body(): logits = jnp.dot(block, head_weight, preferred_element_type=jnp.float32)  23.6 us
    ppermute x12, starting transfers between devices, shifted(): return lax.ppermute(block, axis, route)  21.8 us
    unnamed x1, blocking collectives  11.8 us
  transfers between devices with their start and end apart: 14, of which 6 were waited for; matrix products, arithmetic and copies ran while one was open for 3% of the time, Pallas kernels for 0%

commit v1 on v0

--- a/solution.py
+++ b/solution.py
@@ -146,7 +146,16 @@
     vocabulary_here = head_weight.shape[1]
     first_word = request * vocabulary_here
     columns = jnp.arange(vocabulary_here)
-    block = lax.all_gather(normed, "req", axis=0, tiled=True)
+    ways = lax.axis_size("req")
+    up = [(d, (d + 1) % ways) for d in range(ways)]
+    down = [(d, (d - 1) % ways) for d in range(ways)]
+    earlier, later = ([normed], [normed])
+    for _ in range(ways // 2):
+        earlier.append(lax.ppermute(earlier[-1], "req", up))
+    for _ in range((ways - 1) // 2):
+        later.append(lax.ppermute(later[-1], "req", down))
+    line = jnp.concatenate([*earlier[::-1], *later[1:]], axis=0)
+    block = jnp.roll(line, (lax.axis_index("req") - ways // 2) * normed.shape[0], axis=0)
     words = lax.all_gather(token_ids, "req", axis=0, tiled=True)
     logits = jnp.dot(block, head_weight, preferred_element_type=jnp.float32)
     highest = jnp.max(logits, axis=-1)

time: 363 us -> 386 us (1.063)
  starting transfers between devices: 22.1 us -> 46.2 us
  waiting for transfers between devices: 135 us -> 127 us
  blocking collectives: 133 us -> 138 us
    all_gather x1 -> x0, waiting for transfers between devices: 59.6 us -> none  [body(): block = lax.all_gather(normed, 'req', axis=0, tiled=True)]
    ppermute x0 -> x7, waiting for transfers between devices: none -> 50.7 us  [the longest x4 40.6 us: body(): earlier.append(lax.ppermute(earlier[-1], 'req', up))]
    ppermute x0 -> x7, starting transfers between devices: none -> 24.3 us  [the longest x3 17.7 us: body(): later.append(lax.ppermute(later[-1], 'req', down))]
    unnamed x1, blocking collectives: 11.8 us -> 16.6 us
  transfers between devices with their start and end apart: 14 -> 20, of which waited for: 6 -> 9; matrix products, arithmetic and copies ran while one was open for 3% -> 3% of each run, Pallas kernels for 0% -> 0%
where the time goes in v1:
time: 386 us; the launch traced here: 385 us
  blocking collectives  138 us (36%)
  waiting for transfers between devices  127 us (33%)
  starting transfers between devices  46.2 us (12%)
  matrix products  35.6 us (9%)
  between operations  17.1 us (4%)
  other arithmetic  11.2 us (3%)
  local copies, waits for them, and re-layouts  10 us (3%)
    all_gather x4, blocking collectives, combined_all(): everything = jax.tree.map(lambda part: lax.all_gather(part, axis), shard)  122 us
    reduce_scatter x1, waiting for transfers between devices, body(): lax.psum_scatter(jnp.dot(block, out_weight, preferred_element_type=jnp.fl...  52.2 us
    ppermute x4, waiting for transfers between devices, body(): earlier.append(lax.ppermute(earlier[-1], 'req', up))  40.6 us
    ppermute x12, waiting for transfers between devices, shifted(): return lax.ppermute(block, axis, route)  23.8 us
    dot_general x1, matrix products, body(): logits = jnp.dot(block, head_weight, preferred_element_type=jnp.float32)  23.7 us
    ppermute x12, starting transfers between devices, shifted(): return lax.ppermute(block, axis, route)  21.8 us
    ppermute x3, starting transfers between devices, body(): later.append(lax.ppermute(later[-1], 'req', down))  17.7 us
    unnamed x1, blocking collectives  16.6 us
  transfers between devices with their start and end apart: 20, of which 9 were waited for; matrix products, arithmetic and copies ran while one was open for 3% of the time, Pallas kernels for 0%

profile of v1, /device:TPU:0, one launch (start us, length us, event | category | flops | bytes accessed | tf_op | source)
XLA Modules:
  0.0 385.4 jit_solution(8319802722004875400)
XLA Ops:
  7.2 4.0 %collective-permute-start = (bf16[256,512]{1,0:T(8,128)(2,1)}, bf16[256,512]{1,0:T(8,128)(2,1)S(1)}, u32[]{:S(2)}, u32[]{:S(2)}) collective-permute-start(bf16[256,512]{1,0:T(8,128)(2,1)} %param.16), channel_id=1, source_target_pairs={{20,0},{24,4},{28,8},{0,12},{4,16},{8,20},{12,24},{16,28},{21,1},{... | collective-permute-start | bytes 786440 | tf_op jit(solution)/shard_map/ppermute | solution.py:14
  11.2 1.6 collective-permute-start.1
  12.8 1.5 collective-permute-start.2
  15.7 1.1 constant_dynamic-slice_fusion.6
  16.9 1.0 constant_dynamic-slice_fusion.7
  17.9 1.3 fusion.37
  19.4 1.0 constant_dynamic-slice_fusion.5
  20.5 2.2 constant_dynamic-slice_fusion.4
  23.0 12.6 %collective-permute-done = bf16[256,512]{1,0:T(8,128)(2,1)S(1)} collective-permute-done((bf16[256,512]{1,0:T(8,128)(2,1)}, bf16[256,512]{1,0:T(8,128)(2,1)S(1)}, u32[]{:S(2)}, u32[]{:S(2)}) %collective-permute-start) | collective-permute-done | bytes 262176 | tf_op jit(solution)/shard_map/ppermute | solution.py:14
  35.6 1.6 fusion.4
  37.2 1.9 fusion.5
  39.2 1.1 collective-permute-start.10
  40.3 3.0 collective-permute-start.11
  43.3 1.5 collective-permute-start.3
  45.1 2.0 bitcast_dynamic-update-slice_fusion.3
  47.3 3.2 collective-permute-start.5
  50.5 1.9 collective-permute-start.6
  52.4 2.7 collective-permute-start.7
  55.1 1.0 collective-permute-start.8
  56.7 2.4 collective-permute-done.6
  59.2 5.6 %collective-permute-done.7 = bf16[256,4,128]{2,0,1:T(8,128)(2,1)S(1)} collective-permute-done((bf16[256,4,128]{2,0,1:T(8,128)(2,1)S(1)}, bf16[256,4,128]{2,0,1:T(8,128)(2,1)S(1)}, u32[]{:S(2)}, u32[]{:S(2)}) %collective-permute-start.7) | collective-permute-done | bytes 262176 | tf_op jit(solution)/shard_map/ppermute | solution.py:14
  64.8 3.2 collective-permute-done.8
  68.1 1.3 fusion.7
  69.8 5.4 %fusion.22 = f32[256,4096]{1,0:T(8,128)} fusion(bf16[512,4096]{1,0:T(8,128)(2,1)} %param.21, bf16[32,8,4,128]{3,2,1,0:T(4,128)(2,1)S(1)} %bitcast.136), kind=kOutput, calls=%fused_computation.45 | convolution fusion | flops 1073741824 | bytes 8650752 | tf_op jit(solution)/shard_map/dot_general | solution.py:137
  75.2 52.2 %reduce-scatter.2.cloned.1.call-done = f32[64,4096]{1,0:T(8,128)} async-done(((f32[256,4096]{1,0:T(8,128)}), f32[64,4096]{1,0:T(8,128)}) %reduce-scatter.2.cloned.1.call-update) | async-done | bytes 1048592 | tf_op jit(solution)/shard_map/reduce_scatter | solution.py:136
  127.4 1.5 multiply_reduce_fusion.1
  128.9 1.4 multiply_convert_fusion
  130.3 1.7 collective-permute-start.12
  132.0 14.9 %collective-permute-done.12 = bf16[64,4096]{1,0:T(8,128)(2,1)S(1)} collective-permute-done((bf16[64,4096]{1,0:T(8,128)(2,1)S(1)}, bf16[64,4096]{1,0:T(8,128)(2,1)S(1)}, u32[]{:S(2)}, u32[]{:S(2)}) %collective-permute-start.12) | collective-permute-done | bytes 524320 | tf_op jit(solution)/shard_map/ppermute | solution.py:154
  146.9 4.7 %collective-permute-start.16 = (bf16[64,4096]{1,0:T(8,128)(2,1)S(1)}, bf16[64,4096]{1,0:T(8,128)(2,1)S(1)}, u32[]{:S(2)}, u32[]{:S(2)}) collective-permute-start(bf16[64,4096]{1,0:T(8,128)(2,1)S(1)} %multiply_convert_fusion), channel_id=1, source_target_pairs={{0,28},{4,0},{8,4},{12,8},{16,12},{20,16},{24,20},{28,24},{1,29},{... | collective-permute-start | bytes 1572872 | tf_op jit(solution)/shard_map/ppermute | solution.py:156
  151.6 17.1 %collective-permute-done.13 = bf16[64,4096]{1,0:T(8,128)(2,1)S(1)} collective-permute-done((bf16[64,4096]{1,0:T(8,128)(2,1)S(1)}, bf16[64,4096]{1,0:T(8,128)(2,1)S(1)}, u32[]{:S(2)}, u32[]{:S(2)}) %collective-permute-start.13) | collective-permute-done | bytes 524320 | tf_op jit(solution)/shard_map/ppermute | solution.py:154
  168.7 2.5 collective-permute-start.14
  171.2 12.3 %collective-permute-start.17 = (bf16[64,4096]{1,0:T(8,128)(2,1)S(1)}, bf16[64,4096]{1,0:T(8,128)(2,1)S(1)}, u32[]{:S(2)}, u32[]{:S(2)}) collective-permute-start(bf16[64,4096]{1,0:T(8,128)(2,1)S(1)} %collective-permute-done.16), channel_id=1, source_target_pairs={{0,28},{4,0},{8,4},{12,8},{16,12},{20,16},{24,20},{28,24},{1,29},{... | collective-permute-start | bytes 1572872 | tf_op jit(solution)/shard_map/ppermute | solution.py:156
  183.6 8.7 %collective-permute-done.14 = bf16[64,4096]{1,0:T(8,128)(2,1)S(1)} collective-permute-done((bf16[64,4096]{1,0:T(8,128)(2,1)S(1)}, bf16[64,4096]{1,0:T(8,128)(2,1)S(1)}, u32[]{:S(2)}, u32[]{:S(2)}) %collective-permute-start.14) | collective-permute-done | bytes 524320 | tf_op jit(solution)/shard_map/ppermute | solution.py:154
  192.2 2.5 collective-permute-start.15
  195.4 0.6 dynamic-slice
  196.9 16.6 %all-reduce = s32[512]{0:T(512)S(1)} all-reduce(s32[512]{0:T(512)S(1)} %dynamic-update-slice), channel_id=1, replica_groups=mesh['req'=8,'mp'=4] {'req'}, use_global_device_ids=true, to_apply=%add | all-reduce | flops 512 | bytes 4096
  213.5 0.6 collective-permute-start.18
  214.1 1.1 constant_dynamic-update-slice_fusion.25
  215.5 10.1 %collective-permute-done.18 = bf16[64,4096]{1,0:T(8,128)(2,1)S(1)} collective-permute-done((bf16[64,4096]{1,0:T(8,128)(2,1)S(1)}, bf16[64,4096]{1,0:T(8,128)(2,1)S(1)}, u32[]{:S(2)}, u32[]{:S(2)}) %collective-permute-start.18) | collective-permute-done | bytes 524320 | tf_op jit(solution)/shard_map/ppermute | solution.py:156
  225.6 1.1 constant_dynamic-update-slice_fusion.17
  227.0 23.7 %fusion.38 = (f32[512]{0:T(512)S(1)}, f32[512,4000]{0,1:T(8,128)}) fusion(bf16[4096,4000]{0,1:T(8,128)(2,1)} %param.23, bf16[1024,4096]{1,0:T(8,128)(2,1)S(1)} %constant_dynamic-update-slice_fusion.10, s32[]{:T(128)S(6)} %select_n.205), kind=kOutput, calls=%fused_computation.121 | convolution fusion | flops 16779264000 | bytes 45156356 | tf_op jit(solution)/shard_map/dot_general | solution.py:160
  250.8 4.8 %multiply_reduce_fusion = (f32[512]{0:T(512)S(1)}, f32[512]{0:T(512)S(1)}, f32[512]{0:T(512)S(1)}) fusion(f32[512,4000]{0,1:T(8,128)} %get-tuple-element.271, f32[512]{0:T(512)S(1)} %get-tuple-element.270, s32[512]{0:T(512)S(1)} %broadcast_subtract_fusion), kind=kLoop, calls=%fused_computation.13 | loop fusion | flops 14334464 | bytes 8202240 | tf_op jit(solution)/shard_map/reduce_sum | solution.py:164
  255.7 30.4 %all_gather.19 = f32[8,8,64]{2,1,0:T(8,128)S(1)} all-gather(f32[1,8,64]{2,1,0:T(8,128)S(1)} %all_gather_reshape.15), channel_id=1, replica_groups=mesh['req'=8,'mp'=4] {'req'}, dimensions={0}, use_global_device_ids=true | all-gather | bytes 18432 | tf_op jit(solution)/shard_map/all_gather | solution.py:18
  286.2 30.4 %all_gather.17 = f32[8,8,64]{2,1,0:T(8,128)S(1)} all-gather(f32[1,8,64]{2,1,0:T(8,128)S(1)} %all_gather_reshape.14), channel_id=1, replica_groups=mesh['req'=8,'mp'=4] {'req'}, dimensions={0}, use_global_device_ids=true | all-gather | bytes 18432 | tf_op jit(solution)/shard_map/all_gather | solution.py:18
  316.6 30.4 %all_gather.16 = f32[8,8,64]{2,1,0:T(8,128)S(1)} all-gather(f32[1,8,64]{2,1,0:T(8,128)S(1)} %all_gather_reshape.13), channel_id=1, replica_groups=mesh['req'=8,'mp'=4] {'req'}, dimensions={0}, use_global_device_ids=true | all-gather | bytes 18432 | tf_op jit(solution)/shard_map/all_gather | solution.py:18
  347.1 30.4 %all_gather.15 = f32[8,8,64]{2,1,0:T(8,128)S(1)} all-gather(f32[1,8,64]{2,1,0:T(8,128)S(1)} %all_gather_reshape.12), channel_id=1, replica_groups=mesh['req'=8,'mp'=4] {'req'}, dimensions={0}, use_global_device_ids=true | all-gather | bytes 18432 | tf_op jit(solution)/shard_map/all_gather | solution.py:18
  378.0 0.5 compare_select_fusion
  (104 shorter events, 4.3 us)
Async XLA Ops:
  7.2 8.6 %copy-start = (bf16[2048,2,128]{2,1,0:T(2,128)(2,1)S(1)}, bf16[2048,2,128]{2,1,0:T(2,128)(2,1)}, u32[]{:S(2)}) copy-start(bf16[2048,2,128]{2,1,0:T(2,128)(2,1)} %param.19) | copy-start | bytes 3145732
  7.2 28.5 %copy-start.3 = (bf16[256,512]{1,0:T(8,128)(2,1)S(1)}, bf16[256,512]{1,0:T(8,128)(2,1)}, u32[]{:S(2)}) copy-start(bf16[256,512]{1,0:T(8,128)(2,1)} %param.16) | copy-start | bytes 786436
  7.2 120.2 %reduce-scatter.2.cloned.1.call-start = ((), (), s32[]{:S(2)}) async-start(), calls=%async_computation.1 | async-start | bytes 5242880 | tf_op jit(solution)/shard_map/reduce_scatter | solution.py:136
  7.2 28.4 %collective-permute-start = (bf16[256,512]{1,0:T(8,128)(2,1)}, bf16[256,512]{1,0:T(8,128)(2,1)S(1)}, u32[]{:S(2)}, u32[]{:S(2)}) collective-permute-start(bf16[256,512]{1,0:T(8,128)(2,1)} %param.16), channel_id=1, source_target_pairs={{20,0},{24,4},{28,8},{0,12},{4,16},{8,20},{12,24},{16,28},{21,1},{... | collective-permute-start | bytes 786440 | tf_op jit(solution)/shard_map/ppermute | solution.py:14
  11.2 24.4 %collective-permute-start.1 = (bf16[256,512]{1,0:T(8,128)(2,1)}, bf16[256,512]{1,0:T(8,128)(2,1)S(1)}, u32[]{:S(2)}, u32[]{:S(2)}) collective-permute-start(bf16[256,512]{1,0:T(8,128)(2,1)} %param.16), channel_id=1, source_target_pairs={{24,0},{28,4},{0,8},{4,12},{8,16},{12,20},{16,24},{20,28},{25,1},{... | collective-permute-start | bytes 786440 | tf_op jit(solution)/shard_map/ppermute | solution.py:14
  12.8 22.8 %collective-permute-start.2 = (bf16[256,512]{1,0:T(8,128)(2,1)}, bf16[256,512]{1,0:T(8,128)(2,1)S(1)}, u32[]{:S(2)}, u32[]{:S(2)}) collective-permute-start(bf16[256,512]{1,0:T(8,128)(2,1)} %param.16), channel_id=1, source_target_pairs={{28,0},{0,4},{4,8},{8,12},{12,16},{16,20},{20,24},{24,28},{29,1},{... | collective-permute-start | bytes 786440 | tf_op jit(solution)/shard_map/ppermute | solution.py:14
  39.1 16.0 %collective-permute-start.9 = (f32[256,4]{0,1:T(4,128)S(1)}, f32[256,4]{0,1:T(4,128)S(1)}, u32[]{:S(2)}, u32[]{:S(2)}) collective-permute-start(f32[256,4]{0,1:T(4,128)S(1)} %get-tuple-element.260), channel_id=1, source_target_pairs={{4,0},{8,4},{12,8},{16,12},{20,16},{24,20},{28,24},{0,28},{5,1},{9... | collective-permute-start | bytes 12296 | tf_op jit(solution)/shard_map/ppermute | solution.py:14
  39.2 16.9 %collective-permute-start.10 = (f32[256,4]{0,1:T(4,128)S(1)}, f32[256,4]{0,1:T(4,128)S(1)}, u32[]{:S(2)}, u32[]{:S(2)}) collective-permute-start(f32[256,4]{0,1:T(4,128)S(1)} %get-tuple-element.259), channel_id=1, source_target_pairs={{8,0},{12,4},{16,8},{20,12},{24,16},{28,20},{0,24},{4,28},{9,1},{1... | collective-permute-start | bytes 12296 | tf_op jit(solution)/shard_map/ppermute | solution.py:14
  40.3 15.8 %collective-permute-start.11 = (f32[256,4]{0,1:T(4,128)S(1)}, f32[256,4]{0,1:T(4,128)S(1)}, u32[]{:S(2)}, u32[]{:S(2)}) collective-permute-start(f32[256,4]{0,1:T(4,128)S(1)} %get-tuple-element.258), channel_id=1, source_target_pairs={{12,0},{16,4},{20,8},{24,12},{28,16},{0,20},{4,24},{8,28},{13,1},{... | collective-permute-start | bytes 12296 | tf_op jit(solution)/shard_map/ppermute | solution.py:14
  43.3 4.0 %collective-permute-start.3 = (f32[256,4]{0,1:T(4,128)S(1)}, f32[256,4]{0,1:T(4,128)S(1)}, u32[]{:S(2)}, u32[]{:S(2)}) collective-permute-start(f32[256,4]{0,1:T(4,128)S(1)} %get-tuple-element.263), channel_id=1, source_target_pairs={{4,0},{8,4},{12,8},{16,12},{20,16},{24,20},{28,24},{0,28},{5,1},{9... | collective-permute-start | bytes 12296 | tf_op jit(solution)/shard_map/ppermute | solution.py:14
  44.8 5.7 %collective-permute-start.4 = (f32[256,4]{0,1:T(4,128)S(1)}, f32[256,4]{0,1:T(4,128)S(1)}, u32[]{:S(2)}, u32[]{:S(2)}) collective-permute-start(f32[256,4]{0,1:T(4,128)S(1)} %get-tuple-element.262), channel_id=1, source_target_pairs={{8,0},{12,4},{16,8},{20,12},{24,16},{28,20},{0,24},{4,28},{9,1},{1... | collective-permute-start | bytes 12296 | tf_op jit(solution)/shard_map/ppermute | solution.py:14
  47.3 5.1 %collective-permute-start.5 = (f32[256,4]{0,1:T(4,128)S(1)}, f32[256,4]{0,1:T(4,128)S(1)}, u32[]{:S(2)}, u32[]{:S(2)}) collective-permute-start(f32[256,4]{0,1:T(4,128)S(1)} %get-tuple-element.261), channel_id=1, source_target_pairs={{12,0},{16,4},{20,8},{24,12},{28,16},{0,20},{4,24},{8,28},{13,1},{... | collective-permute-start | bytes 12296 | tf_op jit(solution)/shard_map/ppermute | solution.py:14
  50.5 8.7 %collective-permute-start.6 = (bf16[256,4,128]{2,0,1:T(8,128)(2,1)S(1)}, bf16[256,4,128]{2,0,1:T(8,128)(2,1)S(1)}, u32[]{:S(2)}, u32[]{:S(2)}) collective-permute-start(bf16[256,4,128]{2,0,1:T(8,128)(2,1)S(1)} %get-tuple-element.255), channel_id=1, source_target_pairs={{4,0},{8,4},{12,8},{16,12},{20,16},{24,20},{28,24},{0,28},{5,1},{9... | collective-permute-start | bytes 786440 | tf_op jit(solution)/shard_map/ppermute | solution.py:14
  52.4 12.4 %collective-permute-start.7 = (bf16[256,4,128]{2,0,1:T(8,128)(2,1)S(1)}, bf16[256,4,128]{2,0,1:T(8,128)(2,1)S(1)}, u32[]{:S(2)}, u32[]{:S(2)}) collective-permute-start(bf16[256,4,128]{2,0,1:T(8,128)(2,1)S(1)} %get-tuple-element.254), channel_id=1, source_target_pairs={{8,0},{12,4},{16,8},{20,12},{24,16},{28,20},{0,24},{4,28},{9,1},{1... | collective-permute-start | bytes 786440 | tf_op jit(solution)/shard_map/ppermute | solution.py:14
  55.1 12.9 %collective-permute-start.8 = (bf16[256,4,128]{2,0,1:T(8,128)(2,1)S(1)}, bf16[256,4,128]{2,0,1:T(8,128)(2,1)S(1)}, u32[]{:S(2)}, u32[]{:S(2)}) collective-permute-start(bf16[256,4,128]{2,0,1:T(8,128)(2,1)S(1)} %get-tuple-element.253), channel_id=1, source_target_pairs={{12,0},{16,4},{20,8},{24,12},{28,16},{0,20},{4,24},{8,28},{13,1},{... | collective-permute-start | bytes 786440 | tf_op jit(solution)/shard_map/ppermute | solution.py:14
  69.4 58.0 %copy-start.2 = (bf16[64,4096]{1,0:T(8,128)(2,1)S(1)}, bf16[64,4096]{1,0:T(8,128)(2,1)}, u32[]{:S(2)}) copy-start(bf16[64,4096]{1,0:T(8,128)(2,1)} %param.15) | copy-start | bytes 1572868
  69.8 59.1 %copy-start.4 = (f32[4096]{0:T(1024)S(1)}, f32[4096]{0:T(1024)}, u32[]{:S(2)}) copy-start(f32[4096]{0:T(1024)} %param.22) | copy-start | bytes 49156
  69.8 125.6 %copy-start.6 = (u32[32]{0:T(128)S(1)}, u32[32]{0:T(128)}, u32[]{:S(2)}) copy-start(u32[32]{0:T(128)} %constant.144) | copy-start | bytes 388
  69.8 126.8 %copy-start.5 = (s32[64]{0:T(128)S(1)}, s32[64]{0:T(128)}, u32[]{:S(2)}) copy-start(s32[64]{0:T(128)} %param.24) | copy-start | bytes 772
  130.3 16.6 %collective-permute-start.12 = (bf16[64,4096]{1,0:T(8,128)(2,1)S(1)}, bf16[64,4096]{1,0:T(8,128)(2,1)S(1)}, u32[]{:S(2)}, u32[]{:S(2)}) collective-permute-start(bf16[64,4096]{1,0:T(8,128)(2,1)S(1)} %multiply_convert_fusion), channel_id=1, source_target_pairs={{0,4},{4,8},{8,12},{12,16},{16,20},{20,24},{24,28},{28,0},{1,5},{5... | collective-permute-start | bytes 1572872 | tf_op jit(solution)/shard_map/ppermute | solution.py:154
  146.9 21.8 %collective-permute-start.13 = (bf16[64,4096]{1,0:T(8,128)(2,1)S(1)}, bf16[64,4096]{1,0:T(8,128)(2,1)S(1)}, u32[]{:S(2)}, u32[]{:S(2)}) collective-permute-start(bf16[64,4096]{1,0:T(8,128)(2,1)S(1)} %collective-permute-done.12), channel_id=1, source_target_pairs={{0,4},{4,8},{8,12},{12,16},{16,20},{20,24},{24,28},{28,0},{1,5},{5... | collective-permute-start | bytes 1572872 | tf_op jit(solution)/shard_map/ppermute | solution.py:154
  146.9 24.3 %collective-permute-start.16 = (bf16[64,4096]{1,0:T(8,128)(2,1)S(1)}, bf16[64,4096]{1,0:T(8,128)(2,1)S(1)}, u32[]{:S(2)}, u32[]{:S(2)}) collective-permute-start(bf16[64,4096]{1,0:T(8,128)(2,1)S(1)} %multiply_convert_fusion), channel_id=1, source_target_pairs={{0,28},{4,0},{8,4},{12,8},{16,12},{20,16},{24,20},{28,24},{1,29},{... | collective-permute-start | bytes 1572872 | tf_op jit(solution)/shard_map/ppermute | solution.py:156
  168.7 23.5 %collective-permute-start.14 = (bf16[64,4096]{1,0:T(8,128)(2,1)S(1)}, bf16[64,4096]{1,0:T(8,128)(2,1)S(1)}, u32[]{:S(2)}, u32[]{:S(2)}) collective-permute-start(bf16[64,4096]{1,0:T(8,128)(2,1)S(1)} %collective-permute-done.13), channel_id=1, source_target_pairs={{0,4},{4,8},{8,12},{12,16},{16,20},{20,24},{24,28},{28,0},{1,5},{5... | collective-permute-start | bytes 1572872 | tf_op jit(solution)/shard_map/ppermute | solution.py:154
  171.2 42.3 %collective-permute-start.17 = (bf16[64,4096]{1,0:T(8,128)(2,1)S(1)}, bf16[64,4096]{1,0:T(8,128)(2,1)S(1)}, u32[]{:S(2)}, u32[]{:S(2)}) collective-permute-start(bf16[64,4096]{1,0:T(8,128)(2,1)S(1)} %collective-permute-done.16), channel_id=1, source_target_pairs={{0,28},{4,0},{8,4},{12,8},{16,12},{20,16},{24,20},{28,24},{1,29},{... | collective-permute-start | bytes 1572872 | tf_op jit(solution)/shard_map/ppermute | solution.py:156
  192.2 21.9 %collective-permute-start.15 = (bf16[64,4096]{1,0:T(8,128)(2,1)S(1)}, bf16[64,4096]{1,0:T(8,128)(2,1)}, u32[]{:S(2)}, u32[]{:S(2)}) collective-permute-start(bf16[64,4096]{1,0:T(8,128)(2,1)S(1)} %collective-permute-done.14), channel_id=1, source_target_pairs={{0,4},{4,8},{8,12},{12,16},{16,20},{20,24},{24,28},{28,0},{1,5},{5... | collective-permute-start | bytes 1572872 | tf_op jit(solution)/shard_map/ppermute | solution.py:154
  213.5 12.0 %collective-permute-start.18 = (bf16[64,4096]{1,0:T(8,128)(2,1)S(1)}, bf16[64,4096]{1,0:T(8,128)(2,1)S(1)}, u32[]{:S(2)}, u32[]{:S(2)}) collective-permute-start(bf16[64,4096]{1,0:T(8,128)(2,1)S(1)} %collective-permute-done.17), channel_id=1, source_target_pairs={{0,28},{4,0},{8,4},{12,8},{16,12},{20,16},{24,20},{28,24},{1,29},{... | collective-permute-start | bytes 1572872 | tf_op jit(solution)/shard_map/ppermute | solution.py:156
  227.0 151.5 %copy-start.1 = (bf16[2048,2,128]{2,1,0:T(2,128)(2,1)S(1)}, bf16[2048,2,128]{2,1,0:T(2,128)(2,1)}, u32[]{:S(2)}) copy-start(bf16[2048,2,128]{2,1,0:T(2,128)(2,1)} %param.19) | copy-start | bytes 3145732
Sparse Core Ops, SparseCore 0:
  75.4 51.9 reduce-scatter.1
